TPU v7x, 32 devices: a whole 2x2x4 slice. The times are simulated.
32 devices in a mesh: ctx: 8 (over z, x), exp: 4 (over y, core).
Axes of the slice: x: 2, y: 2, z: 4, core: 2. Of those that a mesh axis runs over, the one named last changes fastest.
Arguments:
- residual: bfloat16 [4, 1024, 2048], P('exp', 'ctx'), may hold values from -54 to 54
- queries: bfloat16 [4, 1024, 2048], P('exp', 'ctx'), may hold values from -160 to 160
- key_states: bfloat16 [4, 1024, 256], P('exp', 'ctx'), may hold values from -6.1 to 6.1
- value_states: bfloat16 [4, 1024, 256], P('exp', 'ctx'), may hold values from -6 to 6
- expert_ids: int32 [4, 1024, 1], P('exp', 'ctx'), may hold values from 0 to 7; in each aligned block of 128 rows (0 to 127, 128 to 255, ..., all dimensions but the last counted through in order) at most 32 rows name the same one
- route_weight: float32 [4, 1024, 1], P('exp', 'ctx'), may hold values from 0.2 to 1
- gate_weight: bfloat16 [4, 8, 192, 2048], P('exp', 'ctx'), may hold values from -0.125 to 0.125
- up_weight: bfloat16 [4, 8, 192, 2048], P('exp', 'ctx'), may hold values from -0.125 to 0.125
- down_weight: bfloat16 [4, 8, 192, 2048], P('exp', 'ctx'), may hold values from -0.21875 to 0.21875
Outputs:
- output: bfloat16 [4, 1024, 2048], P('exp', 'ctx')
Inputs may be any that keep to these rules, and one draw needn't show every extreme that they name: `expert_ids`: within each aligned block of 128 rows (sequence by sequence, positions in order), which is the rows of one device, no expert is named more than 32 times, a bound that some block reaches; every expert is named somewhere.
All inputs are finite; a program needn't handle non-finite values.
Results may differ from a plain program's by a relative error of at most 0.003.
Values may be sent and summed in bfloat16 or wider, within the bound.
No kernel may reach another device: no remote copies, remote signals or barrier semaphores. Data moves between devices by JAX's collectives and lax.ppermute only.
A program may use at most 64 MiB of HBM per device.

v0:
```python
from functools import partial
import math
import jax
import jax.numpy as jnp
from jax import lax
from jax.sharding import PartitionSpec as P

HD = 128
HEADS = 16
KV_HEADS = 2
PIECES = 4
TOPK = 1
negative_fill = -1e30
epsilon = 1e-06


def contract_rows(left_rows, weight_rows):
    return lax.dot_general(
        left_rows, weight_rows, (((1,), (1,)), ((), ())), preferred_element_type=jnp.float32
    )


def to_groups(half_block, heads_kv, group_size, head_dim):
    token_count = half_block.shape[0]
    shaped = half_block.reshape(token_count, heads_kv, group_size, head_dim)
    return jnp.transpose(shaped, (1, 0, 2, 3)).reshape(heads_kv, token_count * group_size, head_dim)


def keep_current(current):
    return current


def block_update(current, query_rows, query_pos, key_block, value_block, key_start, score_scale):
    running_max, running_total, accumulated = current
    scores = (
        jnp.einsum("gqd,kgd->gqk", query_rows, key_block, preferred_element_type=jnp.float32)
        * score_scale
    )
    key_pos = key_start + jnp.arange(key_block.shape[0], dtype=jnp.int32)
    allowed = key_pos[None, None, :] <= query_pos[None, :, None]
    scores = jnp.where(allowed, scores, negative_fill)
    new_max = jnp.maximum(running_max, jnp.max(scores, axis=-1))
    rescale = jnp.exp(running_max - new_max)
    exponent = jnp.where(allowed, jnp.exp(scores - new_max[..., None]), 0.0)
    new_total = running_total * rescale + jnp.sum(exponent, axis=-1)
    product = jnp.einsum(
        "gqk,kgd->gqd",
        exponent.astype(jnp.bfloat16),
        value_block,
        preferred_element_type=jnp.float32,
    )
    return (new_max, new_total, accumulated * rescale[..., None] + product)


def make_folder(query_sets, position_sets, last_positions, heads_kv, head_dim, score_scale):

    def fold_keys(running, key_piece, first_key):
        key_part, value_part = key_piece
        key_count = key_part.shape[1]
        key_width = math.gcd(key_count, 512)
        key_rows = key_part.reshape(key_count, heads_kv, head_dim)
        value_rows = value_part.reshape(key_count, heads_kv, head_dim)

        def one_block(block_index, current_sets):
            offset = block_index * key_width
            key_block = lax.dynamic_slice_in_dim(key_rows, offset, key_width, 0)
            value_block = lax.dynamic_slice_in_dim(value_rows, offset, key_width, 0)
            updated = []
            for current, query_rows, query_pos, last_pos in zip(
                current_sets, query_sets, position_sets, last_positions
            ):
                step_fn = partial(
                    block_update,
                    query_rows=query_rows,
                    query_pos=query_pos,
                    key_block=key_block,
                    value_block=value_block,
                    key_start=offset,
                    score_scale=score_scale,
                )
                updated.append(lax.cond(offset <= last_pos, step_fn, keep_current, current))
            return tuple(updated)

        return lax.fori_loop(0, key_count // key_width, one_block, running)

    return fold_keys


def finish(current, token_count, heads_kv, group_size, head_dim):
    running_max, running_total, accumulated = current
    result = accumulated / running_total[..., None]
    shaped = result.reshape(heads_kv, token_count, group_size, head_dim)
    return (
        jnp.transpose(shaped, (1, 0, 2, 3))
        .reshape(token_count, heads_kv * group_size * head_dim)
        .astype(jnp.bfloat16)
    )


def shards(
    residual,
    queries,
    key_states,
    value_states,
    expert_ids,
    route_weight,
    gate_weight,
    up_weight,
    down_weight,
):
    ctx_count = lax.axis_size("ctx")
    exp_count = lax.axis_size("exp")
    ctx_rank = lax.axis_index("ctx")
    tok_rows = residual.shape[1]
    half_rows = tok_rows // 2
    group_size = HEADS // KV_HEADS
    score_scale = 1.0 / math.sqrt(HD)
    local_queries = queries[0]
    first_half = local_queries[:half_rows]
    second_half = local_queries[half_rows:]
    first_start = ctx_rank * tok_rows
    second_start = first_start + half_rows
    offsets = jnp.repeat(jnp.arange(half_rows, dtype=jnp.int32), group_size)
    query_sets = (
        to_groups(first_half, KV_HEADS, group_size, HD),
        to_groups(second_half, KV_HEADS, group_size, HD),
    )
    position_sets = (first_start + offsets, second_start + offsets)
    last_positions = (first_start + half_rows - 1, second_start + half_rows - 1)
    row_total = half_rows * group_size
    empty_state = (
        jnp.full((KV_HEADS, row_total), negative_fill, jnp.float32),
        jnp.zeros((KV_HEADS, row_total), jnp.float32),
        jnp.zeros((KV_HEADS, row_total, HD), jnp.float32),
    )
    folder = make_folder(query_sets, position_sets, last_positions, KV_HEADS, HD, score_scale)
    final_sets = folder(
        (empty_state, empty_state),
        (
            lax.all_gather(key_states, "ctx", axis=1, tiled=True),
            lax.all_gather(value_states, "ctx", axis=1, tiled=True),
        ),
        jnp.int32(0),
    )
    first_out = finish(final_sets[0], half_rows, KV_HEADS, group_size, HD)
    second_out = finish(final_sets[1], half_rows, KV_HEADS, group_size, HD)
    attention = jnp.concatenate([first_out, second_out], axis=0)
    summed = residual[0].astype(jnp.float32) + lax.optimization_barrier(attention).astype(
        jnp.float32
    )
    normed = (
        summed * lax.rsqrt(jnp.mean(summed * summed, axis=-1, keepdims=True) + epsilon)
    ).astype(jnp.bfloat16)
    width_model = normed.shape[1]
    experts_each = ctx_count // PIECES
    expert_total = experts_each * exp_count
    pair_count = tok_rows * TOPK
    capacity = max(2, 2 * tok_rows * TOPK // expert_total)
    flat_ids = expert_ids[0].reshape(pair_count)
    onehot = (flat_ids[:, None] == jnp.arange(expert_total, dtype=jnp.int32)[None, :]).astype(
        jnp.int32
    )
    earlier = jnp.cumsum(onehot, axis=0) - onehot
    slot_index = jnp.sum(earlier * onehot, axis=1)
    owner_index = flat_ids // experts_each
    local_expert = flat_ids % experts_each
    target = (local_expert * exp_count + owner_index) * capacity + slot_index
    pair_token = jnp.arange(pair_count, dtype=jnp.int32) // TOPK
    slot_total = expert_total * capacity
    slot_table = jnp.full((slot_total,), tok_rows, jnp.int32).at[target].set(pair_token)
    padded = jnp.concatenate([normed, jnp.zeros((1, width_model), jnp.bfloat16)], axis=0)
    outgoing = padded[slot_table].reshape(experts_each, exp_count, capacity, width_model)
    arrived = lax.all_to_all(outgoing, "exp", split_axis=1, concat_axis=1, tiled=True)
    copies = jnp.broadcast_to(
        arrived[:, None], (experts_each, PIECES, exp_count, capacity, width_model)
    ).reshape(ctx_count, exp_count * capacity, width_model)
    gate_piece = gate_weight[0, 0]
    up_piece = up_weight[0, 0]
    down_piece = down_weight[0, 0]
    received = lax.all_to_all(copies, "ctx", split_axis=0, concat_axis=0, tiled=True)
    sources = received.shape[0]
    item_count = received.shape[1]
    flat_rows = received.reshape(sources * item_count, width_model)
    gate_part = contract_rows(flat_rows, gate_piece)
    up_part = contract_rows(flat_rows, up_piece)
    active = (jax.nn.silu(gate_part) * up_part).astype(jnp.bfloat16)
    partial_out = jnp.dot(active, down_piece, preferred_element_type=jnp.float32).astype(
        jnp.bfloat16
    )
    returned = lax.all_to_all(
        partial_out.reshape(sources, item_count, width_model),
        "ctx",
        split_axis=0,
        concat_axis=0,
        tiled=True,
    )
    piece_sum = jnp.sum(
        returned.reshape(experts_each, PIECES, exp_count, capacity, width_model).astype(
            jnp.float32
        ),
        axis=1,
    ).astype(jnp.bfloat16)
    arrived_back = lax.all_to_all(piece_sum, "exp", split_axis=1, concat_axis=1, tiled=True)
    gathered = arrived_back.reshape(slot_total, width_model)[target].astype(jnp.float32)
    weighted = gathered * route_weight[0]
    mixture = jnp.sum(weighted.reshape(tok_rows, TOPK, width_model), axis=1)
    return (summed + mixture).astype(jnp.bfloat16)[None]


def solution(mesh):
    in_specs = (
        P("exp", "ctx", None),
        P("exp", "ctx", None),
        P("exp", "ctx", None),
        P("exp", "ctx", None),
        P("exp", "ctx", None),
        P("exp", "ctx", None),
        P("exp", "ctx", None, None),
        P("exp", "ctx", None, None),
        P("exp", "ctx", None, None),
    )
    out_specs = P("exp", "ctx", None)
    return jax.shard_map(shards, mesh=mesh, in_specs=in_specs, out_specs=out_specs, check_vma=False)
```

profile of v0, /device:TPU:0, one launch (start us, length us, event | category | flops | bytes accessed | tf_op | source)
XLA Modules:
  0.0 328.2 jit_solution(8292580245410848761)
XLA Ops:
  0.0 1.1 slice_bitcast_fusion
  1.4 29.6 %all_gather.6 = bf16[1,1024,256]{1,2,0:T(8,128)(2,1)S(1)} all-gather(bf16[1,128,256]{1,2,0:T(8,128)(2,1)S(1)} %copy.41), channel_id=1, replica_groups=mesh['ctx'=8,'exp'=4] {'ctx'}, dimensions={1}, use_global_device_ids=true | all-gather | bytes 589824 | tf_op jit(solution)/shard_map/all_gather | solution.py:140
  31.1 27.8 %all_gather.7 = bf16[1,1024,256]{1,2,0:T(8,128)(2,1)S(1)} all-gather(bf16[1,128,256]{1,2,0:T(8,128)(2,1)S(1)} %copy.42), channel_id=1, replica_groups=mesh['ctx'=8,'exp'=4] {'ctx'}, dimensions={1}, use_global_device_ids=true | all-gather | bytes 589824 | tf_op jit(solution)/shard_map/all_gather | solution.py:141
  59.0 0.8 broadcast_in_dim.78
  59.8 0.8 broadcast_in_dim.78.clone
  60.6 9.5 %while.24 = (s32[]{:T(128)}, f32[2,512]{1,0:T(2,128)S(1)}, f32[2,512]{1,0:T(2,128)S(1)}, f32[2,512,128]{2,1,0:T(8,128)}, f32[2,512]{1,0:T(2,128)S(1)}, /*index=5...) while((s32[]{:T(128)}, f32[2,512]{1,0:T(2,128)S(1)}, ...), condition=%wide.region_9.10_spmd.clone, body=%wide.region_0.9_spmd.clone.sunk | while | flops 551557120 | bytes 29000316 | solution.py:84
  61.1 3.4 %conditional.7 = ((f32[2,512]{1,0:T(2,128)S(1)}, f32[2,512]{1,0:T(2,128)S(1)}, f32[2,512,128]{2,1,0:T(8,128)})) conditional(s32[]{:T(128)} %convert_element_type.131, (f32[2,512]{1,0:T(2,128)S(1)}, f32[2,512]{1,0:T(2,128)S(1)}, f32[2,512,128]{2,1,0:T(8,128)}) %tuple.67, (s32[]{:T(128)}, s32[]{:T(128)}, bf16[2,512,128]{2,1,0:T(8,128)(2,1)S(1)}, ...), branch_computations={%region_5.5_spmd, %region_6.8_spmd} | conditional | flops 275778560 | bytes 13449312 | solution.py:81
  62.0 0.6 fusion.17
  62.6 1.1 convolution_add_fusion.1
  63.7 0.8 copy-done.6
  64.5 2.6 conditional.6
  65.4 0.6 fusion.6
  66.0 1.1 convolution_add_fusion
  67.1 0.8 copy-done.4
  68.4 1.0 copy-done.3
  69.4 0.8 copy-done.4
  70.2 1.3 fusion.39
  73.5 1.0 scatter_custom_fusion
  74.5 1.4 gather_fusion
  76.0 17.1 %all_to_all.20 = bf16[2,4,32,2048]{3,2,0,1:T(8,128)(2,1)S(1)} all-to-all(bf16[2,4,32,2048]{3,2,0,1:T(8,128)(2,1)S(1)} %copy.49), channel_id=1, replica_groups=mesh['ctx'=8,'exp'=4] {'exp'}, dimensions={1} | all-to-all | bytes 2097152 | tf_op jit(solution)/shard_map/all_to_all | solution.py:173
  93.7 99.7 %all_to_all.21 = bf16[8,128,2048]{2,1,0:T(8,128)(2,1)S(1)} all-to-all(bf16[8,128,2048]{2,1,0:T(8,128)(2,1)S(1)} %bitcast.91), channel_id=1, replica_groups=mesh['ctx'=8,'exp'=4] {'ctx'}, dimensions={0} | all-to-all | bytes 8388608 | tf_op jit(solution)/shard_map/all_to_all | solution.py:180
  193.4 2.0 copy-done.2
  195.4 2.5 fusion.30
  197.9 7.1 %convolution_convert_fusion = bf16[1024,2048]{1,0:T(8,128)(2,1)} fusion(bf16[1024,2048]{1,0:T(8,128)(2,1)} %bitcast.97, bf16[1,1,192,2048]{3,2,1,0:T(8,128)(2,1)S(1)} %copy-done, bf16[1,1,192,2048]{3,2,1,0:T(8,128)(2,1)S(1)} %copy-done.13, f32[1024,192]{0,1:T(8,128)} %fusion.30), kind=kOutput, calls=%fused_computation.43 | convolution fusion | flops 1613889536 | bytes 10747904 | tf_op jit(solution)/shard_map/dot_general | solution.py:187
  205.0 97.0 %all_to_all.22 = bf16[8,128,2048]{2,1,0:T(8,128)(2,1)} all-to-all(bf16[8,128,2048]{2,1,0:T(8,128)(2,1)} %bitcast.98), channel_id=1, replica_groups=mesh['ctx'=8,'exp'=4] {'ctx'}, dimensions={0} | all-to-all | bytes 8388608 | tf_op jit(solution)/shard_map/all_to_all | solution.py:190
  302.0 3.1 reduce_sum.57
  305.0 1.1 copy.51
  306.1 4.2 %all-to-all-start.3 = ((bf16[2,4,32,2048]{3,2,0,1:T(8,128)(2,1)}), bf16[2,4,32,2048]{3,2,0,1:T(8,128)(2,1)}, u32[]{:S(2)}, u32[]{:S(2)}) async-start(bf16[2,4,32,2048]{3,2,0,1:T(8,128)(2,1)} %copy.51), calls=%async_computation.3 | async-start | bytes 2097152 | tf_op jit(solution)/shard_map/all_to_all | solution.py:203
  310.4 14.5 %all-to-all-done.3 = bf16[2,4,32,2048]{3,2,0,1:T(8,128)(2,1)} async-done(((bf16[2,4,32,2048]{3,2,0,1:T(8,128)(2,1)}), bf16[2,4,32,2048]{3,2,0,1:T(8,128)(2,1)}, u32[]{:S(2)}, u32[]{:S(2)}) %all-to-all-start.3) | async-done | bytes 1048608 | tf_op jit(solution)/shard_map/all_to_all | solution.py:203
  324.9 1.3 copy.52
  326.2 0.9 gather_fusion.1
  327.1 1.1 fusion.37
  (85 shorter events, 5.6 us)
Async XLA Ops:
  0.0 197.9 %copy-start = (bf16[1,1,192,2048]{3,2,1,0:T(8,128)(2,1)S(1)}, bf16[1,1,192,2048]{3,2,1,0:T(8,128)(2,1)}, u32[]{:S(2)}) copy-start(bf16[1,1,192,2048]{3,2,1,0:T(8,128)(2,1)} %param.23) | copy-start | bytes 2359300
  0.0 1.3 copy-start.8
  0.0 30.9 %copy-start.9 = (bf16[1,128,256]{2,1,0:T(8,128)(2,1)S(1)}, bf16[1,128,256]{2,1,0:T(8,128)(2,1)}, u32[]{:S(2)}) copy-start(bf16[1,128,256]{2,1,0:T(8,128)(2,1)} %param.18) | copy-start | bytes 196612
  61.1 3.4 %copy-start.3 = (f32[2,512,128]{2,1,0:T(8,128)S(1)}, f32[2,512,128]{2,1,0:T(8,128)}, u32[]{:S(2)}) copy-start(f32[2,512,128]{2,1,0:T(8,128)} %get-tuple-element.613) | copy-start | bytes 1572868 | tf_op jit(solution)/shard_map/while
  61.5 1.2 copy-start.5
  63.7 0.8 copy-start.6
  67.1 0.8 copy-start.4
  68.3 1.0 copy-start.3
  69.4 0.8 copy-start.4
  70.2 1.5 copy-start.7
  71.5 1.0 copy-start.1
  71.9 1.1 copy-start.10
  93.7 101.7 %copy-start.12 = (bf16[1,1,192,2048]{3,2,1,0:T(8,128)(2,1)S(1)}, bf16[1,1,192,2048]{3,2,1,0:T(8,128)(2,1)}, u32[]{:S(2)}) copy-start(bf16[1,1,192,2048]{3,2,1,0:T(8,128)(2,1)} %param.21) | copy-start | bytes 2359300
  193.4 2.0 copy-start.2
  195.4 2.5 copy-start.13
  306.1 18.8 %all-to-all-start.3 = ((bf16[2,4,32,2048]{3,2,0,1:T(8,128)(2,1)}), bf16[2,4,32,2048]{3,2,0,1:T(8,128)(2,1)}, u32[]{:S(2)}, u32[]{:S(2)}) async-start(bf16[2,4,32,2048]{3,2,0,1:T(8,128)(2,1)} %copy.51), calls=%async_computation.3 | async-start | bytes 2097152 | tf_op jit(solution)/shard_map/all_to_all | solution.py:203
  326.2 1.0 copy-start.11
where the time goes:
time: 329 us; the launch traced here: 328 us
  blocking collectives  271 us (82%)
  local copies, waits for them, and re-layouts  16.7 us (5%)
  waiting for transfers between devices  14.5 us (4%)
  matrix products  12.8 us (4%)
  other arithmetic  8.21 us (2%)
  starting transfers between devices  4.23 us (1%)
    all_to_all x1, blocking collectives, shards(): lax.all_to_all(copies, 'ctx', split_axis=0, concat_axis=0, tiled=True)  99.7 us
    all_to_all x1, blocking collectives, shards(): lax.all_to_all(partial_out.reshape(sources, item_count, width_model), 'ct...  97 us
    all_gather x1, blocking collectives, shards(): lax.all_gather(key_states, 'ctx', axis=1, tiled=True)  29.6 us
    all_gather x1, blocking collectives, shards(): lax.all_gather(value_states, 'ctx', axis=1, tiled=True)  27.8 us
    all_to_all x1, blocking collectives, shards(): lax.all_to_all(outgoing, 'exp', split_axis=1, concat_axis=1, tiled=True)  17.1 us
    all_to_all x1, waiting for transfers between devices, shards(): lax.all_to_all(piece_sum, 'exp', split_axis=1, concat_axis=1, tiled=True)  14.5 us
    dot_general x1, matrix products, shards(): jnp.dot(active, down_piece, preferred_element_type=jnp.float32)  7.06 us
  transfers between devices with their start and end apart: 1, of which 1 were waited for; matrix products, arithmetic and copies ran while one was open for 0% of the time, Pallas kernels for 0%

commit v1 on v0

--- a/solution.py
+++ b/solution.py
@@ -12,6 +12,40 @@
 TOPK = 1
 negative_fill = -1e30
 epsilon = 1e-06
+
+
+def shape_the_block(panel, along_dim, vec):
+    odd, work_now = (panel.shape[:along_dim], panel.shape[along_dim + 1 :])
+    res = panel.reshape(*odd, vec, -1, *work_now)
+    spare = jnp.moveaxis(res, along_dim, 0)
+    return spare
+
+
+def handle_thing(w_in, array_axis):
+    w_in = jnp.moveaxis(w_in, 0, array_axis)
+    oldest = w_in.shape
+    n_now = w_in.reshape(
+        *oldest[:array_axis], oldest[array_axis] * oldest[array_axis + 1], *oldest[array_axis + 2 :]
+    )
+    return n_now
+
+
+def ranges_lead(raw, device_axis, load, vals):
+    vec_out = lax.psum(1, axis_name=device_axis)
+    u1 = lax.axis_index(device_axis)
+    met_up, p_next = (vec_out, u1)
+    carry_out = shape_the_block(raw, load, met_up)
+    pool = [carry_out[p_next]]
+    for k in range(1, met_up):
+        big = carry_out[p_next ^ k]
+        a_next = lax.ppermute(
+            big, axis_name=device_axis, perm=[(it, it ^ k) for it in range(met_up)]
+        )
+        pool.append(a_next)
+    g_now = jnp.stack(pool, axis=0)
+    carry_out = g_now[p_next ^ jnp.arange(met_up)]
+    y2 = handle_thing(carry_out, vals)
+    return y2
 
 
 def contract_rows(left_rows, weight_rows):
@@ -170,7 +204,7 @@
     slot_table = jnp.full((slot_total,), tok_rows, jnp.int32).at[target].set(pair_token)
     padded = jnp.concatenate([normed, jnp.zeros((1, width_model), jnp.bfloat16)], axis=0)
     outgoing = padded[slot_table].reshape(experts_each, exp_count, capacity, width_model)
-    arrived = lax.all_to_all(outgoing, "exp", split_axis=1, concat_axis=1, tiled=True)
+    arrived = ranges_lead(outgoing, "exp", 1, 1)
     copies = jnp.broadcast_to(
         arrived[:, None], (experts_each, PIECES, exp_count, capacity, width_model)
     ).reshape(ctx_count, exp_count * capacity, width_model)

time: 329 us -> 329 us (level)
  blocking collectives: 271 us -> 255 us
  waiting for transfers between devices: 14.5 us -> 26.5 us
    all_to_all x1 -> x0, blocking collectives: 17.1 us -> none  [shards(): lax.all_to_all(outgoing, 'exp', split_axis=1, concat_axis=1, tiled=True)]
    ppermute x0 -> x3, waiting for transfers between devices: none -> 12 us  [ranges_lead(): lax.ppermute(big, axis_name=device_axis, perm=[(it, it ^ k) for it in ran...]
  transfers between devices with their start and end apart: 1 -> 4, of which waited for: 1 -> 3; matrix products, arithmetic and copies ran while one was open for 0% -> 0% of each run, Pallas kernels for 0% -> 0%
where the time goes in v1:
time: 329 us
  blocking collectives  255 us (78%)
  waiting for transfers between devices  26.5 us (8%)
  local copies, waits for them, and re-layouts  19.5 us (6%)
  matrix products  12.8 us (4%)
  other arithmetic  8.35 us (3%)
  starting transfers between devices  6.17 us (2%)
    all_to_all x1, blocking collectives, shards(): lax.all_to_all(copies, 'ctx', split_axis=0, concat_axis=0, tiled=True)  100 us
    all_to_all x1, blocking collectives, shards(): lax.all_to_all(partial_out.reshape(sources, item_count, width_model), 'ct...  97.2 us
    all_gather x1, blocking collectives, shards(): lax.all_gather(key_states, 'ctx', axis=1, tiled=True)  29.6 us
    all_gather x1, blocking collectives, shards(): lax.all_gather(value_states, 'ctx', axis=1, tiled=True)  27.8 us
    all_to_all x1, waiting for transfers between devices, shards(): lax.all_to_all(piece_sum, 'exp', split_axis=1, concat_axis=1, tiled=True)  14.5 us
    ppermute x3, waiting for transfers between devices, ranges_lead(): lax.ppermute(big, axis_name=device_axis, perm=[(it, it ^ k) for it in ran...  12 us
    dot_general x1, matrix products, shards(): jnp.dot(active, down_piece, preferred_element_type=jnp.float32)  7.06 us
  transfers between devices with their start and end apart: 4, of which 3 were waited for; matrix products, arithmetic and copies ran while one was open for 0% of the time, Pallas kernels for 0%

profile of v1, /device:TPU:0, one launch (start us, length us, event | category | flops | bytes accessed | tf_op | source)
XLA Modules:
  0.0 328.9 jit_solution(16171580885751667377)
XLA Ops:
  0.0 1.2 slice_bitcast_fusion
  1.4 29.6 %all_gather.6 = bf16[1,1024,256]{1,2,0:T(8,128)(2,1)S(1)} all-gather(bf16[1,128,256]{1,2,0:T(8,128)(2,1)S(1)} %copy.51), channel_id=1, replica_groups=mesh['ctx'=8,'exp'=4] {'ctx'}, dimensions={1}, use_global_device_ids=true | all-gather | bytes 589824 | tf_op jit(solution)/shard_map/all_gather | solution.py:174
  31.1 27.8 %all_gather.7 = bf16[1,1024,256]{1,2,0:T(8,128)(2,1)S(1)} all-gather(bf16[1,128,256]{1,2,0:T(8,128)(2,1)S(1)} %copy.52), channel_id=1, replica_groups=mesh['ctx'=8,'exp'=4] {'ctx'}, dimensions={1}, use_global_device_ids=true | all-gather | bytes 589824 | tf_op jit(solution)/shard_map/all_gather | solution.py:175
  59.0 0.8 broadcast_in_dim.80
  59.8 0.8 broadcast_in_dim.80.clone
  60.7 9.5 %while.24 = (s32[]{:T(128)}, f32[2,512]{1,0:T(2,128)S(1)}, f32[2,512]{1,0:T(2,128)S(1)}, f32[2,512,128]{2,1,0:T(8,128)}, f32[2,512]{1,0:T(2,128)S(1)}, /*index=5...) while((s32[]{:T(128)}, f32[2,512]{1,0:T(2,128)S(1)}, ...), condition=%wide.region_9.10_spmd.clone, body=%wide.region_0.9_spmd.clone.sunk | while | flops 551557120 | bytes 29000316 | solution.py:118
  61.1 3.4 %conditional.7 = ((f32[2,512]{1,0:T(2,128)S(1)}, f32[2,512]{1,0:T(2,128)S(1)}, f32[2,512,128]{2,1,0:T(8,128)})) conditional(s32[]{:T(128)} %convert_element_type.131, (f32[2,512]{1,0:T(2,128)S(1)}, f32[2,512]{1,0:T(2,128)S(1)}, f32[2,512,128]{2,1,0:T(8,128)}) %tuple.71, (s32[]{:T(128)}, s32[]{:T(128)}, bf16[2,512,128]{2,1,0:T(8,128)(2,1)S(1)}, ...), branch_computations={%region_5.5_spmd, %region_6.8_spmd} | conditional | flops 275778560 | bytes 13449312 | solution.py:115
  62.7 1.1 convolution_add_fusion.1
  63.8 0.8 copy-done.6
  64.6 2.6 conditional.6
  66.1 1.1 convolution_add_fusion
  68.4 1.0 copy-done.3
  70.2 1.3 fusion.39
  73.5 1.0 scatter_custom_fusion
  74.6 1.4 gather_fusion
  76.1 1.6 collective-permute-start.1
  78.0 7.3 %collective-permute-done.1 = bf16[2,1,32,2048]{3,2,0,1:T(8,128)(2,1)S(1)} collective-permute-done((bf16[2,1,32,2048]{3,2,0,1:T(8,128)(2,1)S(1)}, bf16[2,1,32,2048]{3,2,0,1:T(8,128)(2,1)S(1)}, u32[]{:S(2)}, u32[]{:S(2)}) %collective-permute-start.1) | collective-permute-done | bytes 262176 | tf_op jit(solution)/shard_map/ppermute | solution.py:41
  85.3 4.7 %collective-permute-done.2 = bf16[2,1,32,2048]{3,2,0,1:T(8,128)(2,1)S(1)} collective-permute-done((bf16[2,1,32,2048]{3,2,0,1:T(8,128)(2,1)S(1)}, bf16[2,1,32,2048]{3,2,0,1:T(8,128)(2,1)S(1)}, u32[]{:S(2)}, u32[]{:S(2)}) %collective-permute-start.2) | collective-permute-done | bytes 262176 | tf_op jit(solution)/shard_map/ppermute | solution.py:41
  90.1 1.6 gather_fusion.1
  91.7 1.3 copy_bitcast_fusion
  93.6 100.3 %all_to_all.15 = bf16[8,128,2048]{2,1,0:T(8,128)(2,1)S(1)} all-to-all(bf16[8,128,2048]{2,1,0:T(8,128)(2,1)S(1)} %bitcast.113), channel_id=1, replica_groups=mesh['ctx'=8,'exp'=4] {'ctx'}, dimensions={0} | all-to-all | bytes 8388608 | tf_op jit(solution)/shard_map/all_to_all | solution.py:214
  193.9 2.0 copy-done.2
  195.9 2.5 fusion.30
  198.4 7.1 %convolution_convert_fusion = bf16[1024,2048]{1,0:T(8,128)(2,1)} fusion(bf16[1024,2048]{1,0:T(8,128)(2,1)} %bitcast.119, bf16[1,1,192,2048]{3,2,1,0:T(8,128)(2,1)S(1)} %copy-done, bf16[1,1,192,2048]{3,2,1,0:T(8,128)(2,1)S(1)} %copy-done.13, f32[1024,192]{0,1:T(8,128)} %fusion.30), kind=kOutput, calls=%fused_computation.44 | convolution fusion | flops 1613889536 | bytes 10747904 | tf_op jit(solution)/shard_map/dot_general | solution.py:221
  205.4 97.2 %all_to_all.16 = bf16[8,128,2048]{2,1,0:T(8,128)(2,1)} all-to-all(bf16[8,128,2048]{2,1,0:T(8,128)(2,1)} %bitcast.120), channel_id=1, replica_groups=mesh['ctx'=8,'exp'=4] {'ctx'}, dimensions={0} | all-to-all | bytes 8388608 | tf_op jit(solution)/shard_map/all_to_all | solution.py:224
  302.6 3.1 reduce_sum.57
  305.7 1.1 copy.60
  306.8 4.2 %all-to-all-start.2 = ((bf16[2,4,32,2048]{3,2,0,1:T(8,128)(2,1)}), bf16[2,4,32,2048]{3,2,0,1:T(8,128)(2,1)}, u32[]{:S(2)}, u32[]{:S(2)}) async-start(bf16[2,4,32,2048]{3,2,0,1:T(8,128)(2,1)} %copy.60), calls=%async_computation.2 | async-start | bytes 2097152 | tf_op jit(solution)/shard_map/all_to_all | solution.py:237
  311.0 14.5 %all-to-all-done.2 = bf16[2,4,32,2048]{3,2,0,1:T(8,128)(2,1)} async-done(((bf16[2,4,32,2048]{3,2,0,1:T(8,128)(2,1)}), bf16[2,4,32,2048]{3,2,0,1:T(8,128)(2,1)}, u32[]{:S(2)}, u32[]{:S(2)}) %all-to-all-start.2) | async-done | bytes 1048608 | tf_op jit(solution)/shard_map/all_to_all | solution.py:237
  325.6 1.3 copy.61
  326.9 0.9 gather_fusion.2
  327.8 1.1 fusion.37
  (94 shorter events, 8.8 us)
Async XLA Ops:
  0.0 198.4 %copy-start = (bf16[1,1,192,2048]{3,2,1,0:T(8,128)(2,1)S(1)}, bf16[1,1,192,2048]{3,2,1,0:T(8,128)(2,1)}, u32[]{:S(2)}) copy-start(bf16[1,1,192,2048]{3,2,1,0:T(8,128)(2,1)} %param.23) | copy-start | bytes 2359300
  0.0 1.3 copy-start.8
  0.0 31.0 %copy-start.9 = (bf16[1,128,256]{2,1,0:T(8,128)(2,1)S(1)}, bf16[1,128,256]{2,1,0:T(8,128)(2,1)}, u32[]{:S(2)}) copy-start(bf16[1,128,256]{2,1,0:T(8,128)(2,1)} %param.18) | copy-start | bytes 196612
  61.1 3.4 %copy-start.3 = (f32[2,512,128]{2,1,0:T(8,128)S(1)}, f32[2,512,128]{2,1,0:T(8,128)}, u32[]{:S(2)}) copy-start(f32[2,512,128]{2,1,0:T(8,128)} %get-tuple-element.632) | copy-start | bytes 1572868 | tf_op jit(solution)/shard_map/while
  61.5 1.2 copy-start.5
  63.7 0.8 copy-start.6
  67.2 0.8 copy-start.4
  68.4 1.0 copy-start.3
  69.4 0.8 copy-start.4
  70.2 1.5 copy-start.7
  71.5 1.0 copy-start.1
  71.9 1.1 copy-start.10
  76.0 2.0 collective-permute-start
  76.1 9.2 %collective-permute-start.1 = (bf16[2,1,32,2048]{3,2,0,1:T(8,128)(2,1)S(1)}, bf16[2,1,32,2048]{3,2,0,1:T(8,128)(2,1)S(1)}, u32[]{:S(2)}, u32[]{:S(2)}) collective-permute-start(bf16[2,1,32,2048]{3,2,0,1:T(8,128)(2,1)S(1)} %get-tuple-element.485), channel_id=1, source_target_pairs={{0,2},{1,3},{2,0},{3,1},{4,6},{5,7},{6,4},{7,5},{8,10},{9,11},{10,... | collective-permute-start | bytes 786440 | tf_op jit(solution)/shard_map/ppermute | solution.py:41
  77.7 12.3 %collective-permute-start.2 = (bf16[2,1,32,2048]{3,2,0,1:T(8,128)(2,1)S(1)}, bf16[2,1,32,2048]{3,2,0,1:T(8,128)(2,1)S(1)}, u32[]{:S(2)}, u32[]{:S(2)}) collective-permute-start(bf16[2,1,32,2048]{3,2,0,1:T(8,128)(2,1)S(1)} %get-tuple-element.484), channel_id=1, source_target_pairs={{0,3},{1,2},{2,1},{3,0},{4,7},{5,6},{6,5},{7,4},{8,11},{9,10},{10,... | collective-permute-start | bytes 786440 | tf_op jit(solution)/shard_map/ppermute | solution.py:41
  93.6 102.3 %copy-start.12 = (bf16[1,1,192,2048]{3,2,1,0:T(8,128)(2,1)S(1)}, bf16[1,1,192,2048]{3,2,1,0:T(8,128)(2,1)}, u32[]{:S(2)}) copy-start(bf16[1,1,192,2048]{3,2,1,0:T(8,128)(2,1)} %param.21) | copy-start | bytes 2359300
  193.9 2.0 copy-start.2
  195.8 2.5 copy-start.13
  306.8 18.8 %all-to-all-start.2 = ((bf16[2,4,32,2048]{3,2,0,1:T(8,128)(2,1)}), bf16[2,4,32,2048]{3,2,0,1:T(8,128)(2,1)}, u32[]{:S(2)}, u32[]{:S(2)}) async-start(bf16[2,4,32,2048]{3,2,0,1:T(8,128)(2,1)} %copy.60), calls=%async_computation.2 | async-start | bytes 2097152 | tf_op jit(solution)/shard_map/all_to_all | solution.py:237
  326.9 1.0 copy-start.11
